TPU v7x, 256 devices: a whole 4x4x8 slice. The times are simulated.
256 devices in a mesh: dp: 8 (over z_hi, core), expert: 32 (over x, z_lo, y).
Axes of the slice: x: 4, y: 4, z: 8 (z_hi: 4, z_lo: 2; z = z_hi * 2 + z_lo), core: 2. Of those that a mesh axis runs over, the one named last changes fastest.
Arguments:
- tokens: bfloat16 [256, 256, 1024], P(('dp', 'expert'))
- router: bfloat16 [1024, 128], replicated
- weight_in: bfloat16 [128, 1024, 2048], P('expert', None, 'dp'), may hold values from -0.1875 to 0.1875
- weight_out: bfloat16 [128, 2048, 1024], P('expert', 'dp'), may hold values from -0.125 to 0.125
- cotangent: bfloat16 [256, 256, 1024], P(('dp', 'expert')), may hold values from -6 to 6
Outputs:
- mixed: bfloat16 [256, 256, 1024], P(('dp', 'expert'))
- grad_tokens: bfloat16 [256, 256, 1024], P(('dp', 'expert'))
- grad_router: float32 [1024, 128], replicated
- grad_weight_in: bfloat16 [128, 1024, 2048], P('expert', None, 'dp')
- grad_weight_out: bfloat16 [128, 2048, 1024], P('expert', 'dp')
All inputs are finite; a program needn't handle non-finite values.
Results may differ from a plain program's by a relative error of at most 0.018.
Values may be sent and summed in bfloat16 or wider, within the bound.
A program may use at most 64 MiB of HBM per device.

v0:
```python
import jax
import jax.numpy as jnp
from jax import lax
from jax.sharding import PartitionSpec as P


def gelu_exact(values):
    return jax.nn.gelu(values, approximate=False)


def local(tokens, router, weight_in, weight_out, cotangent):
    experts_dev = weight_in.shape[0]
    width = tokens.shape[2]
    logits = jnp.einsum("isd,de->ise", tokens, router, preferred_element_type=jnp.float32)
    dispatch_prob = jax.nn.softmax(logits, axis=1)
    combine_prob = jax.nn.softmax(logits, axis=2)
    dispatch = dispatch_prob.astype(jnp.bfloat16)
    combine = combine_prob.astype(jnp.bfloat16)
    slots = jnp.einsum("ise,isd->ied", dispatch, tokens, preferred_element_type=jnp.float32).astype(
        jnp.bfloat16
    )
    grad_slots = jnp.einsum(
        "ise,isd->ied", combine, cotangent, preferred_element_type=jnp.float32
    ).astype(jnp.bfloat16)

    def to_owners(local_rows):
        arrived = lax.all_to_all(local_rows, "expert", split_axis=1, concat_axis=1, tiled=True)
        return lax.all_gather(arrived, "dp", axis=0, tiled=True)

    def from_owners(partial_value):
        summed = lax.psum_scatter(partial_value, "dp", scatter_dimension=0, tiled=True).astype(
            jnp.float32
        )
        return lax.all_to_all(
            summed.astype(jnp.bfloat16), "expert", split_axis=1, concat_axis=1, tiled=True
        )

    slot_rows = to_owners(slots)
    blocks = slot_rows.reshape(-1, experts_dev, width)
    pre_act = jnp.einsum("rkd,kdf->rkf", blocks, weight_in, preferred_element_type=jnp.float32)
    hidden = gelu_exact(pre_act).astype(jnp.bfloat16)
    partial_value = jnp.einsum(
        "rkf,kfd->rkd", hidden, weight_out, preferred_element_type=jnp.float32
    )
    blocks, pre_act, hidden, partial_value = (
        blocks,
        pre_act,
        hidden,
        partial_value.astype(jnp.bfloat16).reshape(slot_rows.shape),
    )
    expert_outs = from_owners(partial_value)
    grad_rows = to_owners(grad_slots)
    grad_blocks = grad_rows.reshape(blocks.shape)
    grad_hidden = jnp.einsum(
        "rkd,kfd->rkf", grad_blocks, weight_out, preferred_element_type=jnp.float32
    )
    _, gelu_back = jax.vjp(gelu_exact, pre_act)
    grad_pre = gelu_back(grad_hidden)[0].astype(jnp.bfloat16)
    grad_second = jnp.einsum(
        "rkf,rkd->kfd", hidden, grad_blocks, preferred_element_type=jnp.float32
    ).astype(jnp.bfloat16)
    grad_first = jnp.einsum(
        "rkd,rkf->kdf", blocks, grad_pre, preferred_element_type=jnp.float32
    ).astype(jnp.bfloat16)
    partial_back = jnp.einsum(
        "rkf,kdf->rkd", grad_pre, weight_in, preferred_element_type=jnp.float32
    )
    grad_first, grad_second, partial_back = (
        grad_first,
        grad_second,
        partial_back.astype(jnp.bfloat16).reshape(grad_rows.shape),
    )
    grad_slot_all = from_owners(partial_back)
    mixed = jnp.einsum(
        "ise,ied->isd", combine, expert_outs, preferred_element_type=jnp.float32
    ).astype(jnp.bfloat16)
    grad_comb = jnp.einsum(
        "isd,ied->ise", cotangent, expert_outs, preferred_element_type=jnp.float32
    )
    grad_disp = jnp.einsum(
        "isd,ied->ise", tokens, grad_slot_all, preferred_element_type=jnp.float32
    )
    part_disp = dispatch_prob * (
        grad_disp - jnp.sum(dispatch_prob * grad_disp, axis=1, keepdims=True)
    )
    part_comb = combine_prob * (
        grad_comb - jnp.sum(combine_prob * grad_comb, axis=2, keepdims=True)
    )
    grad_logits = (part_disp + part_comb).astype(jnp.bfloat16)
    grad_tokens = (
        jnp.einsum("ise,ied->isd", dispatch, grad_slot_all, preferred_element_type=jnp.float32)
        + jnp.einsum("ise,de->isd", grad_logits, router, preferred_element_type=jnp.float32)
    ).astype(jnp.bfloat16)
    router_term = jnp.einsum("isd,ise->de", tokens, grad_logits, preferred_element_type=jnp.float32)
    grad_router = lax.psum(router_term, ("dp", "expert"))
    return (mixed, grad_tokens, grad_router, grad_first, grad_second)


def solution(mesh):
    return jax.shard_map(
        local,
        mesh=mesh,
        in_specs=(
            P(("dp", "expert"), None, None),
            P(),
            P("expert", None, "dp"),
            P("expert", "dp", None),
            P(("dp", "expert"), None, None),
        ),
        out_specs=(
            P(("dp", "expert"), None, None),
            P(("dp", "expert"), None, None),
            P(),
            P("expert", None, "dp"),
            P("expert", "dp", None),
        ),
        check_vma=False,
    )
```

profile of v0, /device:TPU:2, one launch (start us, length us, event | category | flops | bytes accessed | tf_op | source)
XLA Modules:
  0.0 497.0 jit_solution(17294189357701382762)
XLA Ops:
  11.3 2.1 reduce.12
  13.6 16.7 %all_to_all.20 = bf16[32,2,2048]{2,1,0:T(2,128)(2,1)S(1)} all-to-all(bf16[32,2,2048]{2,1,0:T(2,128)(2,1)S(1)} %reshape.119), channel_id=1, replica_groups=mesh['dp'=8,'expert'=32] {'expert'}, dimensions={0} | all-to-all | bytes 524288 | tf_op jit(solution)/shard_map/all_to_all | solution.py:27
  32.3 2.2 reduce.14
  34.6 12.8 %all_to_all.21 = bf16[32,2,2048]{2,1,0:T(2,128)(2,1)S(1)} all-to-all(bf16[32,2,2048]{2,1,0:T(2,128)(2,1)S(1)} %reshape.123), channel_id=1, replica_groups=mesh['dp'=8,'expert'=32] {'expert'}, dimensions={0} | all-to-all | bytes 524288 | tf_op jit(solution)/shard_map/all_to_all | solution.py:27
  48.7 18.3 %all-gather.3.cloned.1.call-done = bf16[8,128,1024]{2,1,0:T(8,128)(2,1)} async-done(((bf16[1,128,1024]{2,1,0:T(8,128)(2,1)}), bf16[8,128,1024]{2,1,0:T(8,128)(2,1)}) %all-gather.3.cloned.1.call-update) | async-done | bytes 2097168 | tf_op jit(solution)/shard_map/all_gather | solution.py:28
  67.0 4.1 reshape.112
  71.1 4.3 copy.53
  75.4 5.3 %fusion.13 = (bf16[256,4,256]{2,0,1:T(8,128)(2,1)S(1)}, f32[4,256,256]{2,1,0:T(8,128)}) fusion(bf16[256,4,1024]{0,2,1:T(8,128)(2,1)} %copy.53, bf16[4,1024,256]{2,1,0:T(8,128)(2,1)S(1)} %copy-done), kind=kOutput, calls=%fused_computation.29 | convolution fusion | flops 553910272 | bytes 5767168 | tf_op jit(solution)/shard_map/rkd,kdf->rkf/dot_general | solution.py:40
  80.7 23.0 %all-gather.5.cloned.1.call-done = bf16[8,128,1024]{2,1,0:T(8,128)(2,1)} async-done(((bf16[1,128,1024]{2,1,0:T(8,128)(2,1)}), bf16[8,128,1024]{2,1,0:T(8,128)(2,1)}) %all-gather.5.cloned.1.call-update) | async-done | bytes 2097168 | tf_op jit(solution)/shard_map/all_gather | solution.py:28
  103.7 4.1 reshape.116
  107.8 5.7 %fusion.19 = bf16[256,4,256]{2,0,1:T(8,128)(2,1)S(1)} fusion(bf16[4,256,1024]{2,1,0:T(8,128)(2,1)} %param.8, bf16[256,4,1024]{2,1,0:T(4,128)(2,1)} %reshape.116, f32[4,256,256]{2,1,0:T(8,128)} %get-tuple-element.33), kind=kOutput, calls=%fused_computation.35 | convolution fusion | flops 555745280 | bytes 5767168 | tf_op jit(solution)/shard_map/rkd,kfd->rkf/dot_general | solution.py:54
  114.3 2.9 copy.49
  117.2 4.0 reshape.117
  121.5 2.3 convert_bitcast_fusion.1
  123.8 2.9 copy.44
  126.8 3.9 reshape.113
  130.7 31.9 %reduce-scatter.5.cloned.1.call-done = bf16[1,128,1024]{2,1,0:T(8,128)(2,1)} async-done(((bf16[8,128,1024]{2,1,0:T(8,128)(2,1)}), bf16[1,128,1024]{2,1,0:T(8,128)(2,1)}) %reduce-scatter.5.cloned.1.call-update) | async-done | bytes 262160 | tf_op jit(solution)/shard_map/reduce_scatter | solution.py:31
  162.6 2.1 copy.92
  164.8 3.1 reduce.15
  168.8 7.7 %all-to-all-start.3 = ((bf16[32,2,2048]{2,1,0:T(2,128)(2,1)}), bf16[32,2,2048]{2,1,0:T(2,128)(2,1)S(1)}, u32[]{:S(2)}, u32[]{:S(2)}) async-start(bf16[32,2,2048]{2,1,0:T(2,128)(2,1)} %reshape.125), calls=%async_computation.5 | async-start | bytes 524288 | tf_op jit(solution)/shard_map/all_to_all | solution.py:34
  176.5 4.5 convolution_convert_fusion
  181.0 28.3 %reduce-scatter.3.cloned.1.call-done = bf16[1,128,1024]{2,1,0:T(8,128)(2,1)} async-done(((bf16[8,128,1024]{2,1,0:T(8,128)(2,1)}), bf16[1,128,1024]{2,1,0:T(8,128)(2,1)}) %reduce-scatter.3.cloned.1.call-update) | async-done | bytes 262160 | tf_op jit(solution)/shard_map/reduce_scatter | solution.py:31
  210.7 2.9 reduce.13
  213.5 1.8 reshape.121
  215.4 7.4 %all-to-all-start.1 = ((bf16[32,2,2048]{2,1,0:T(2,128)(2,1)}), bf16[32,2,2048]{2,1,0:T(2,128)(2,1)}, u32[]{:S(2)}, u32[]{:S(2)}) async-start(bf16[32,2,2048]{2,1,0:T(2,128)(2,1)} %reshape.121), calls=%async_computation.2 | async-start | bytes 524288 | tf_op jit(solution)/shard_map/all_to_all | solution.py:34
  223.1 3.6 convolution_convert_fusion.1
  229.0 1.8 all-to-all-done.1
  230.8 2.8 reshape.122
  238.7 2.2 fusion.7
  240.9 2.2 fusion.8
  243.1 245.3 %all-reduce.2.cloned.1.call-done = f32[1024,128]{0,1:T(8,128)} async-done(((f32[1024,128]{0,1:T(8,128)}), f32[1024,128]{0,1:T(8,128)}) %all-reduce.2.cloned.1.call-update) | async-done | bytes 524304 | tf_op jit(solution)/shard_map/psum | solution.py:95
  488.4 2.0 copy.56
  (48 shorter events, 18.5 us)
Async XLA Ops:
  7.2 68.3 %copy-start = (bf16[4,1024,256]{2,1,0:T(8,128)(2,1)S(1)}, bf16[4,1024,256]{2,1,0:T(8,128)(2,1)}, u32[]{:S(2)}) copy-start(bf16[4,1024,256]{2,1,0:T(8,128)(2,1)} %param.7) | copy-start | bytes 6291460
  7.2 59.8 %all-gather.3.cloned.1.call-start = ((), (), s32[]{:S(2)}) async-start(), calls=%async_computation.6 | async-start | bytes 2359296 | tf_op jit(solution)/shard_map/all_gather | solution.py:28
  10.4 21.1 %copy-start.1 = (bf16[1,256,1024]{2,1,0:T(8,128)(2,1)S(1)}, bf16[1,256,1024]{2,1,0:T(8,128)(2,1)}, u32[]{:S(2)}) copy-start(bf16[1,256,1024]{2,1,0:T(8,128)(2,1)} %param.9) | copy-start | bytes 1572868
  31.4 72.2 %all-gather.5.cloned.1.call-start = ((), (), s32[]{:S(2)}) async-start(), calls=%async_computation.8 | async-start | bytes 2359296 | tf_op jit(solution)/shard_map/all_gather | solution.py:28
  48.5 114.1 %reduce-scatter.5.cloned.1.call-start = ((), (), s32[]{:S(2)}) async-start(), calls=%async_computation.9 | async-start | bytes 2359296 | tf_op jit(solution)/shard_map/reduce_scatter | solution.py:31
  121.2 88.1 %reduce-scatter.3.cloned.1.call-start = ((), (), s32[]{:S(2)}) async-start(), calls=%async_computation.7 | async-start | bytes 2359296 | tf_op jit(solution)/shard_map/reduce_scatter | solution.py:31
  168.8 46.6 %all-to-all-start.3 = ((bf16[32,2,2048]{2,1,0:T(2,128)(2,1)}), bf16[32,2,2048]{2,1,0:T(2,128)(2,1)S(1)}, u32[]{:S(2)}, u32[]{:S(2)}) async-start(bf16[32,2,2048]{2,1,0:T(2,128)(2,1)} %reshape.125), calls=%async_computation.5 | async-start | bytes 524288 | tf_op jit(solution)/shard_map/all_to_all | solution.py:34
  215.4 15.4 %all-to-all-start.1 = ((bf16[32,2,2048]{2,1,0:T(2,128)(2,1)}), bf16[32,2,2048]{2,1,0:T(2,128)(2,1)}, u32[]{:S(2)}, u32[]{:S(2)}) async-start(bf16[32,2,2048]{2,1,0:T(2,128)(2,1)} %reshape.121), calls=%async_computation.2 | async-start | bytes 524288 | tf_op jit(solution)/shard_map/all_to_all | solution.py:34
  222.8 265.6 %all-reduce.2.cloned.1.call-start = ((), (), s32[]{:S(2)}) async-start(), calls=%async_computation.10 | async-start | bytes 1048576 | tf_op jit(solution)/shard_map/psum | solution.py:95
  233.6 3.9 copy-start.2
  235.2 1.6 copy-start.4
  235.2 5.7 %copy-start.3 = (bf16[1024,128]{1,0:T(8,128)(2,1)S(1)}, bf16[1024,128]{1,0:T(8,128)(2,1)}, u32[]{:S(2)}) copy-start(bf16[1024,128]{1,0:T(8,128)(2,1)} %param.6) | copy-start | bytes 786436
  236.8 0.7 copy-start.5
  236.8 0.7 copy-start.6
  236.8 0.6 copy-start.7
Sparse Core Ops, SparseCore 0:
  31.6 35.4 all-gather.2
  69.5 34.1 all-gather.4
  121.4 41.2 reduce-scatter.4
  165.6 43.6 reduce-scatter.2
  238.8 249.5 all-reduce.1
where the time goes:
time: 498 us; the launch traced here: 497 us
  waiting for transfers between devices  349 us (70%)
  local copies, waits for them, and re-layouts  42.7 us (9%)
  matrix products  35.6 us (7%)
  blocking collectives  29.5 us (6%)
  starting transfers between devices  16 us (3%)
  between operations  14 us (3%)
  other arithmetic  10.5 us (2%)
    psum x1, waiting for transfers between devices, local(): grad_router = lax.psum(router_term, ('dp', 'expert'))  245 us
    reduce_scatter x2, waiting for transfers between devices, from_owners(): lax.psum_scatter(partial_value, 'dp', scatter_dimension=0, tiled=True)  60.2 us
    all_gather x2, waiting for transfers between devices, to_owners(): return lax.all_gather(arrived, 'dp', axis=0, tiled=True)  41.3 us
    all_to_all x2, blocking collectives, to_owners(): lax.all_to_all(local_rows, 'expert', split_axis=1, concat_axis=1, tiled=T...  29.5 us
    all_to_all x2, starting transfers between devices, from_owners(): lax.all_to_all(summed.astype(jnp.bfloat16), 'expert', split_axis=1, conca...  15.1 us
    unnamed x26, local copies, waits for them, and re-layouts  10.5 us
    unnamed x4, other arithmetic  10.3 us
  transfers between devices with their start and end apart: 7, of which 6 were waited for; matrix products, arithmetic and copies ran while one was open for 11% of the time, Pallas kernels for 0%

commit v1 on v0

--- a/solution.py
+++ b/solution.py
@@ -92,7 +92,9 @@
         + jnp.einsum("ise,de->isd", grad_logits, router, preferred_element_type=jnp.float32)
     ).astype(jnp.bfloat16)
     router_term = jnp.einsum("isd,ise->de", tokens, grad_logits, preferred_element_type=jnp.float32)
-    grad_router = lax.psum(router_term, ("dp", "expert"))
+    grad_router = router_term
+    for over in ("expert", "dp"):
+        grad_router = lax.psum(grad_router, over)
     return (mixed, grad_tokens, grad_router, grad_first, grad_second)
 
 

time: 498 us -> 617 us (1.24)
  waiting for transfers between devices: 349 us -> 469 us
    psum x1 -> x2, waiting for transfers between devices: 245 us -> 372 us  [local(): grad_router = lax.psum(grad_router, over)]
    all_gather x2, waiting for transfers between devices: 41.3 us -> 33.4 us  [to_owners(): return lax.all_gather(arrived, 'dp', axis=0, tiled=True)]
  transfers between devices with their start and end apart: 7 -> 8, of which waited for: 6 -> 7; matrix products, arithmetic and copies ran while one was open for 11% -> 11% of each run, Pallas kernels for 0% -> 0%
where the time goes in v1:
time: 617 us; the launch traced here: 616 us
  waiting for transfers between devices  469 us (76%)
  local copies, waits for them, and re-layouts  43.5 us (7%)
  matrix products  31.6 us (5%)
  blocking collectives  29.5 us (5%)
  starting transfers between devices  16.4 us (3%)
  between operations  14.3 us (2%)
  other arithmetic  11.6 us (2%)
    psum x2, waiting for transfers between devices, local(): grad_router = lax.psum(grad_router, over)  372 us
    reduce_scatter x2, waiting for transfers between devices, from_owners(): lax.psum_scatter(partial_value, 'dp', scatter_dimension=0, tiled=True)  58.2 us
    all_gather x2, waiting for transfers between devices, to_owners(): return lax.all_gather(arrived, 'dp', axis=0, tiled=True)  33.4 us
    all_to_all x2, blocking collectives, to_owners(): lax.all_to_all(local_rows, 'expert', split_axis=1, concat_axis=1, tiled=T...  29.5 us
    all_to_all x2, starting transfers between devices, from_owners(): lax.all_to_all(summed.astype(jnp.bfloat16), 'expert', split_axis=1, conca...  15.5 us
  transfers between devices with their start and end apart: 8, of which 7 were waited for; matrix products, arithmetic and copies ran while one was open for 11% of the time, Pallas kernels for 0%

profile of v1, /device:TPU:2, one launch (start us, length us, event | category | flops | bytes accessed | tf_op | source)
XLA Modules:
  0.0 616.0 jit_solution(365408758710342228)
XLA Ops:
  11.4 2.2 reduce.12
  13.7 16.7 %all_to_all.20 = bf16[32,2,2048]{2,1,0:T(2,128)(2,1)S(1)} all-to-all(bf16[32,2,2048]{2,1,0:T(2,128)(2,1)S(1)} %reshape.119), channel_id=1, replica_groups=mesh['dp'=8,'expert'=32] {'expert'}, dimensions={0} | all-to-all | bytes 524288 | tf_op jit(solution)/shard_map/all_to_all | solution.py:27
  32.4 2.2 reduce.14
  34.8 12.8 %all_to_all.21 = bf16[32,2,2048]{2,1,0:T(2,128)(2,1)S(1)} all-to-all(bf16[32,2,2048]{2,1,0:T(2,128)(2,1)S(1)} %reshape.123), channel_id=1, replica_groups=mesh['dp'=8,'expert'=32] {'expert'}, dimensions={0} | all-to-all | bytes 524288 | tf_op jit(solution)/shard_map/all_to_all | solution.py:27
  48.8 18.3 %all-gather.3.cloned.1.call-done = bf16[8,128,1024]{2,1,0:T(8,128)(2,1)} async-done(((bf16[1,128,1024]{2,1,0:T(8,128)(2,1)}), bf16[8,128,1024]{2,1,0:T(8,128)(2,1)}) %all-gather.3.cloned.1.call-update) | async-done | bytes 2097168 | tf_op jit(solution)/shard_map/all_gather | solution.py:28
  67.1 4.1 reshape.112
  71.2 4.3 copy.53
  75.5 5.5 fusion.13
  81.7 2.9 copy.44
  84.7 4.0 reshape.113
  88.9 15.1 %all-gather.5.cloned.1.call-done = bf16[8,128,1024]{2,1,0:T(8,128)(2,1)} async-done(((bf16[1,128,1024]{2,1,0:T(8,128)(2,1)}), bf16[8,128,1024]{2,1,0:T(8,128)(2,1)}) %all-gather.5.cloned.1.call-update) | async-done | bytes 2097168 | tf_op jit(solution)/shard_map/all_gather | solution.py:28
  104.0 4.1 reshape.116
  108.1 5.7 fusion.19
  114.6 2.9 copy.49
  117.6 4.0 reshape.117
  121.5 26.2 %reduce-scatter.3.cloned.1.call-done = bf16[1,128,1024]{2,1,0:T(8,128)(2,1)} async-done(((bf16[8,128,1024]{2,1,0:T(8,128)(2,1)}), bf16[1,128,1024]{2,1,0:T(8,128)(2,1)}) %reduce-scatter.3.cloned.1.call-update) | async-done | bytes 262160 | tf_op jit(solution)/shard_map/reduce_scatter | solution.py:31
  147.8 2.1 copy.94
  149.9 3.2 reduce.13
  153.9 7.3 %all-to-all-start.1 = ((bf16[32,2,2048]{2,1,0:T(2,128)(2,1)}), bf16[32,2,2048]{2,1,0:T(2,128)(2,1)S(1)}, u32[]{:S(2)}, u32[]{:S(2)}) async-start(bf16[32,2,2048]{2,1,0:T(2,128)(2,1)} %reshape.121), calls=%async_computation.2 | async-start | bytes 524288 | tf_op jit(solution)/shard_map/all_to_all | solution.py:34
  161.3 32.0 %reduce-scatter.5.cloned.1.call-done = bf16[1,128,1024]{2,1,0:T(8,128)(2,1)} async-done(((bf16[8,128,1024]{2,1,0:T(8,128)(2,1)}), bf16[1,128,1024]{2,1,0:T(8,128)(2,1)}) %reduce-scatter.5.cloned.1.call-update) | async-done | bytes 262160 | tf_op jit(solution)/shard_map/reduce_scatter | solution.py:31
  193.2 2.1 copy.92
  195.4 3.9 reduce.15
  199.3 1.8 reshape.125
  201.1 8.2 %all-to-all-start.3 = ((bf16[32,2,2048]{2,1,0:T(2,128)(2,1)}), bf16[32,2,2048]{2,1,0:T(2,128)(2,1)}, u32[]{:S(2)}, u32[]{:S(2)}) async-start(bf16[32,2,2048]{2,1,0:T(2,128)(2,1)} %reshape.125), calls=%async_computation.5 | async-start | bytes 524288 | tf_op jit(solution)/shard_map/all_to_all | solution.py:34
  212.1 5.2 all-to-all-done.3
  217.3 2.8 reshape.126
  222.2 2.2 convolution_bitcast_fusion
  224.5 4.6 convolution_convert_fusion
  229.2 2.0 convolution_convert_fusion.1
  231.2 291.5 %all-reduce.3.cloned.1.call-done = f32[1024,128]{0,1:T(8,128)} async-done(((f32[1024,128]{0,1:T(8,128)}), f32[1024,128]{0,1:T(8,128)}) %all-reduce.3.cloned.1.call-update) | async-done | bytes 524304 | tf_op jit(solution)/shard_map/psum | solution.py:97
  526.5 80.6 %all-reduce.5.cloned.1.call-done = f32[1024,128]{0,1:T(8,128)} async-done(((f32[1024,128]{0,1:T(8,128)}), f32[1024,128]{0,1:T(8,128)}) %all-reduce.5.cloned.1.call-update) | async-done | bytes 524304 | tf_op jit(solution)/shard_map/psum | solution.py:97
  607.1 2.0 copy.56
  (55 shorter events, 19.0 us)
Async XLA Ops:
  7.2 68.3 %copy-start = (bf16[4,1024,256]{2,1,0:T(8,128)(2,1)S(1)}, bf16[4,1024,256]{2,1,0:T(8,128)(2,1)}, u32[]{:S(2)}) copy-start(bf16[4,1024,256]{2,1,0:T(8,128)(2,1)} %param.7) | copy-start | bytes 6291460
  7.2 59.9 %all-gather.3.cloned.1.call-start = ((), (), s32[]{:S(2)}) async-start(), calls=%async_computation.6 | async-start | bytes 2359296 | tf_op jit(solution)/shard_map/all_gather | solution.py:28
  10.4 21.2 %copy-start.2 = (bf16[1,256,1024]{2,1,0:T(8,128)(2,1)S(1)}, bf16[1,256,1024]{2,1,0:T(8,128)(2,1)}, u32[]{:S(2)}) copy-start(bf16[1,256,1024]{2,1,0:T(8,128)(2,1)} %param.9) | copy-start | bytes 1572868
  31.5 72.5 %all-gather.5.cloned.1.call-start = ((), (), s32[]{:S(2)}) async-start(), calls=%async_computation.8 | async-start | bytes 2359296 | tf_op jit(solution)/shard_map/all_gather | solution.py:28
  48.6 99.2 %reduce-scatter.3.cloned.1.call-start = ((), (), s32[]{:S(2)}) async-start(), calls=%async_computation.7 | async-start | bytes 2359296 | tf_op jit(solution)/shard_map/reduce_scatter | solution.py:31
  75.5 5.5 copy-start.4
  88.7 104.6 %reduce-scatter.5.cloned.1.call-start = ((), (), s32[]{:S(2)}) async-start(), calls=%async_computation.9 | async-start | bytes 2359296 | tf_op jit(solution)/shard_map/reduce_scatter | solution.py:31
  153.9 47.1 %all-to-all-start.1 = ((bf16[32,2,2048]{2,1,0:T(2,128)(2,1)}), bf16[32,2,2048]{2,1,0:T(2,128)(2,1)S(1)}, u32[]{:S(2)}, u32[]{:S(2)}) async-start(bf16[32,2,2048]{2,1,0:T(2,128)(2,1)} %reshape.121), calls=%async_computation.2 | async-start | bytes 524288 | tf_op jit(solution)/shard_map/all_to_all | solution.py:34
  201.1 16.2 %all-to-all-start.3 = ((bf16[32,2,2048]{2,1,0:T(2,128)(2,1)}), bf16[32,2,2048]{2,1,0:T(2,128)(2,1)}, u32[]{:S(2)}, u32[]{:S(2)}) async-start(bf16[32,2,2048]{2,1,0:T(2,128)(2,1)} %reshape.125), calls=%async_computation.5 | async-start | bytes 524288 | tf_op jit(solution)/shard_map/all_to_all | solution.py:34
  209.3 313.5 %all-reduce.3.cloned.1.call-start = ((), (), s32[]{:S(2)}) async-start(), calls=%async_computation.10 | async-start | bytes 1048576 | tf_op jit(solution)/shard_map/psum | solution.py:97
  221.6 0.6 copy-start.6
  221.6 0.6 copy-start.8
  224.5 382.7 %all-reduce.5.cloned.1.call-start = ((), (), s32[]{:S(2)}) async-start(), calls=%async_computation.11 | async-start | bytes 1048576 | tf_op jit(solution)/shard_map/psum | solution.py:97
  224.5 4.7 copy-start.1
  229.2 293.6 %copy-start.3 = (bf16[128,1,1024]{2,1,0:T(2,128)(2,1)S(1)}, bf16[128,1,1024]{2,1,0:T(2,128)(2,1)}, u32[]{:S(2)}) copy-start(bf16[128,1,1024]{2,1,0:T(2,128)(2,1)} %reshape.122) | copy-start | bytes 786436
  231.2 294.1 %copy-start.5 = (bf16[1024,128]{1,0:T(8,128)(2,1)S(1)}, bf16[1024,128]{1,0:T(8,128)(2,1)}, u32[]{:S(2)}) copy-start(bf16[1024,128]{1,0:T(8,128)(2,1)} %param.6) | copy-start | bytes 786436
  231.2 294.1 %copy-start.7 = (f32[256]{0:T(256)S(1)}, f32[256]{0:T(256)}, u32[]{:S(2)}) copy-start(f32[256]{0:T(256)} %copy-done.6) | copy-start | bytes 3076
  231.2 294.1 %copy-start.9 = (f32[128]{0:T(128)S(1)}, f32[128]{0:T(128)}, u32[]{:S(2)}) copy-start(f32[128]{0:T(128)} %copy-done.8) | copy-start | bytes 1540
Sparse Core Ops, SparseCore 0:
  31.7 35.4 all-gather.2
  69.6 34.4 all-gather.4
  106.6 41.1 reduce-scatter.2
  150.2 43.0 reduce-scatter.4
  224.6 298.1 all-reduce.2
  525.4 81.6 all-reduce.4
